TPU v7x, 32 devices: a whole 2x2x4 slice. The times are simulated.
32 devices in a mesh: tx: 2 (over x), box: 16 (over z, y, core).
Axes of the slice: x: 2, y: 2, z: 4, core: 2. Of those that a mesh axis runs over, the one named last changes fastest.
Arguments:
- contrast_tangent: bfloat16 [16, 128], P('box', 'tx'), may hold values from -6 to 6
- incident: bfloat16 [64, 16, 128], P('tx', 'box'), may hold values from -6 to 6
- background: bfloat16 [16, 128], P('box'), may hold values from -3 to 3
- counts: int32 [16], P('box'), may hold values from 1 to 64, as said below
- box_mats: bfloat16 [16, 16384, 128], P('box'), may hold values from -0.046875 to 0.046875
- centers: float32 [3, 16], replicated, may hold values from -8 to 8
Outputs:
- hessian_product: float32 [16, 128], P('box', 'tx')
Inputs may be any that keep to these rules, and one draw needn't show every extreme that they name: Each box's occupied voxels are the first counts slots of its 64; some box is full and some holds one voxel.
All inputs are finite; a program needn't handle non-finite values.
Results may differ from a plain program's by a relative error of at most 0.004.
Values may be sent and summed in bfloat16 or wider, within the bound.
No kernel may reach another device: no remote copies, remote signals or barrier semaphores. Data moves between devices by JAX's collectives and lax.ppermute only.
A program may use at most 64 MiB of HBM per device.

v0:
```python
import functools

import jax
import jax.numpy as jnp
from jax import lax
from jax.experimental import pallas as pl
from jax.experimental.pallas import tpu as pltpu
from jax.sharding import PartitionSpec as P


F32 = jnp.float32
BF16 = jnp.bfloat16
VMEM = pl.BlockSpec(memory_space=pltpu.VMEM)
SMEM = pl.BlockSpec(memory_space=pltpu.SMEM)
GRANT = 12 << 20
SMALL = 2 << 20
WHOLE = 60 << 20
CONTRACT_LAST = (((1,), (1,)), ((), ()))


def bits_below(total):
    assert total & (total - 1) == 0
    return [1 << k for k in range(total.bit_length() - 1)]


def turned(values):
    return pltpu.roll(values, values.shape[-1] // 2, axis=values.ndim - 1)


def slice_kernel(total, ids_ref, planes_ref, *refs):
    outs, sems = refs[:total], refs[total]
    size = outs[0].shape[1]
    copies = []
    for other in reversed(range(total)):
        chunk = ids_ref[0] * total + ((ids_ref[1] ^ other) & (total - 1))
        source = planes_ref.at[:, pl.ds(pl.multiple_of(chunk * size, size), size), :]
        copies.append(pltpu.make_async_copy(source, outs[other], sems.at[other]))
    for copy in copies:
        copy.start()
    for copy in copies:
        copy.wait()


def pack_kernel(tx_total, ids_ref, counts_ref, incident_ref, tangent_ref, backdrop_ref, out_ref):
    each, width = incident_ref.shape
    out_ref[0, :each, :] = incident_ref[...]
    shape = (out_ref.shape[1] - each, width)
    row = lax.broadcasted_iota(jnp.int32, shape, 0)
    lane = lax.broadcasted_iota(jnp.int32, shape, 1)
    tangent = jnp.concatenate([tangent_ref[...].astype(F32)] * tx_total, axis=-1)
    first = ids_ref[0] * (width // tx_total)
    mine = (lane >= first) & (lane < first + width // tx_total)
    half = width // 2
    slot = jnp.where(lane < half, lane, lane - half)
    facts = jnp.where((row == 0) & mine, jnp.broadcast_to(tangent, shape), 0.0)
    facts = jnp.where(row == 1, jnp.broadcast_to(backdrop_ref[...].astype(F32), shape), facts)
    facts = jnp.where(row == 2, jnp.where(slot < counts_ref[0], 1.0, 0.0), facts)
    out_ref[0, each:, :] = facts.astype(BF16)


def join_kernel(left_ref, right_ref, out_ref):
    at = left_ref.shape[0]
    out_ref[:at] = left_ref[...]
    out_ref[at:] = right_ref[...]


def phase_kernel(group, total, ids_ref, centers_ref, cos_ref, sin_ref, phase_ref):
    size = cos_ref.shape[0]
    chunk = ids_ref[0] * group + (ids_ref[1] & (group - 1))
    sample_ids = chunk * size + lax.broadcasted_iota(jnp.int32, (1, size), 1)
    height = 1.0 - (2.0 * sample_ids.astype(F32) + 1.0) / total
    radial = jnp.sqrt(1.0 - height * height)
    turn_ids = lax.rem(sample_ids * 1597, jnp.full_like(sample_ids, 4181))
    azimuth = 2.0 * jnp.pi / 4181.0 * turn_ids.astype(F32)
    along_x, along_y = radial * jnp.cos(azimuth), radial * jnp.sin(azimuth)
    for j in range(group):
        box = ids_ref[1] ^ j
        phase_ref[j : j + 1] = jnp.pi * (
            centers_ref[0, box] * along_x + centers_ref[1, box] * along_y + centers_ref[2, box] * height
        )
    cos_ref[...] = jnp.cos(phase_ref[...]).T
    sin_ref[...] = jnp.sin(phase_ref[...]).T


def turn_rows(rows_ref, piece_ref, cos_ref, sin_ref, j):
    samples, width = piece_ref.shape[1:]
    lanes = slice(j * width, (j + 1) * width)
    cos_j, sin_j = cos_ref[:, j : j + 1], sin_ref[:, j : j + 1]
    real, imag = piece_ref[0].astype(F32), piece_ref[1].astype(F32)
    rows_ref[:samples, lanes] = (cos_j * real - sin_j * imag).astype(BF16)
    rows_ref[samples:, lanes] = (sin_j * real + cos_j * imag).astype(BF16)


def fill_kernel(group, planes, each, *refs):
    pieces = refs[: group - 1]
    cos_ref, sin_ref = refs[group - 1 : group + 1]
    packed = refs[group + 1 : group + 1 + group // 2]
    rows_ref, source_ref, coef_ref, top_ref, late_ref, flat_ref = refs[group + 1 + group // 2 :]
    width = pieces[0].shape[2]
    low = lax.broadcasted_iota(jnp.int32, (1, width), 1) < width // 2
    for j in range(group):
        lanes = slice(j * width, (j + 1) * width)
        if j < group - 1:
            turn_rows(rows_ref, pieces[j], cos_ref, sin_ref, j)

        def fact(plane):
            return packed[j // 2][plane * 2 + j % 2, each:, :].astype(F32)

        def factors(value, live):
            other = turned(value)
            return jnp.where(low, value, other) * live, jnp.where(low, -other, value) * live

        facts = fact(0)
        live = facts[2:3]
        tangent = facts[0:1]
        for plane in range(1, planes):
            tangent = tangent + fact(plane)[0:1]
        straight, crossed = factors(tangent, live)
        if j % 2 == 0:
            kept = factors(facts[1:2], live)
            coef_ref[0, j // 2 : j // 2 + 1] = kept[0]
            coef_ref[1, j // 2 : j // 2 + 1] = kept[1]
        for plane in range(planes):
            field = packed[j // 2][plane * 2 + j % 2, :each, :].astype(F32)
            value = (field * straight + turned(field) * crossed).astype(BF16)
            if j % 2 == 0:
                source_ref[(plane * group + j) // 2] = value
            if j < group - 1:
                flat_ref[plane * each : (plane + 1) * each, lanes] = value
            else:
                late_ref[plane * each : (plane + 1) * each] = value
    ready = (group - 1) * width
    top_ref[...] = lax.dot_general(
        flat_ref[...], rows_ref[:, :ready], CONTRACT_LAST, preferred_element_type=F32
    )


def finish_kernel(group, piece_ref, cos_ref, sin_ref, late_ref, part_ref, _, rows_ref, top_ref, send_ref):
    turn_rows(rows_ref, piece_ref, cos_ref, sin_ref, group - 1)
    lanes = slice((group - 1) * piece_ref.shape[2], group * piece_ref.shape[2])
    top = part_ref[...] + lax.dot_general(
        late_ref[...], rows_ref[:, lanes], CONTRACT_LAST, preferred_element_type=F32
    )
    top_ref[...] = top
    send_ref[...] = top.astype(BF16)


def back_kernel(group, top_ref, other_ref, rows_ref, part_ref, send_ref, *whole_ref):
    planes, each, width = part_ref.shape[0] * 2 // group, part_ref.shape[1], part_ref.shape[2]
    returned = (top_ref[...] + other_ref[...].astype(F32)).astype(BF16)
    part = jnp.dot(returned, rows_ref[...], preferred_element_type=F32)
    for plane in range(planes):
        for j in range(group):
            at = plane * group + j
            block = part[plane * each : (plane + 1) * each, j * width : (j + 1) * width]
            if j % 2:
                send_ref[at // 2] = block.astype(BF16)
            else:
                part_ref[at // 2] = block
            if whole_ref:
                whole_ref[0][at] = block


def source_kernel(group, bit, conj, part_ref, other_ref, coef_ref, *refs):
    out_ref = refs[-1]
    for at in range(part_ref.shape[0]):
        jj = at % (group // 2)
        field = part_ref[at] + other_ref[at ^ bit].astype(F32)
        straight = field * coef_ref[0, jj : jj + 1]
        crossed = turned(field) * coef_ref[1, jj : jj + 1]
        value = straight - crossed if conj else refs[0][at].astype(F32) + (straight + crossed)
        out_ref[at] = value.astype(BF16)


def top_kernel(group, even_ref, odd_ref, rows_ref, top_ref, send_ref, flat_ref):
    planes, each, width = even_ref.shape[0] * 2 // group, even_ref.shape[1], even_ref.shape[2]
    for plane in range(planes):
        for j in range(group):
            block = (odd_ref if j % 2 else even_ref)[(plane * group + j) // 2]
            flat_ref[plane * each : (plane + 1) * each, j * width : (j + 1) * width] = block
    top = lax.dot_general(flat_ref[...], rows_ref[...], CONTRACT_LAST, preferred_element_type=F32)
    top_ref[...] = top
    send_ref[...] = top.astype(BF16)


def last_kernel(group, planes, each, top_ref, other_ref, rows_ref, part_ref, *refs):
    packed, out_ref = refs[:-1], refs[-1]
    width = part_ref.shape[2]
    returned = (top_ref[...] + other_ref[...].astype(F32)).astype(BF16)
    part = jnp.dot(returned, rows_ref[...], preferred_element_type=F32)
    low = lax.broadcasted_iota(jnp.int32, (1, width), 1) < width // 2
    for j in range(group):
        same = jnp.zeros((1, width), F32)
        cross = jnp.zeros((1, width), F32)
        for plane in range(planes):
            block = part[plane * each : (plane + 1) * each, j * width : (j + 1) * width]
            block = block + part_ref[plane * group + j]
            field = packed[j // 2][plane * 2 + j % 2, :each, :].astype(F32)
            same = same + jnp.sum(field * block, axis=0, keepdims=True)
            cross = cross + jnp.sum(field * turned(block), axis=0, keepdims=True)
        out_ref[j : j + 1] = jnp.where(low, same + turned(same), turned(cross) - cross)


def shards(contrast_tangent, incident, background, counts, box_mats, centers):
    tx_total, box_total = lax.axis_size("tx"), lax.axis_size("box")
    tx_id, box_id = lax.axis_index("tx"), lax.axis_index("box")
    group = max(box_total // 2, 1)
    halves = box_total // group
    members = tx_total * group
    each, width = incident.shape[0], incident.shape[2]
    count = tx_total * each
    matrix = box_mats[0]
    samples = matrix.shape[0] // 2
    piece = samples // members
    box_bits = bits_below(group)
    tx_bits = [bit * group for bit in bits_below(tx_total)]

    def swap(value, tx_bit, box_bit):
        pairs = [
            (t * box_total + b, (t ^ tx_bit) * box_total + (b ^ box_bit))
            for t in range(tx_total)
            for b in range(box_total)
        ]
        return lax.ppermute(value, ("tx", "box"), pairs)

    def swap_member(value, bit):
        return swap(value, bit // group, bit % group)

    def call(kernel, outs, ins, scratch=(), specs=None, grant=GRANT, cost=None, aliases={}):
        return pl.pallas_call(
            kernel,
            out_shape=outs,
            in_specs=specs or [VMEM] * len(ins),
            out_specs=jax.tree.map(lambda _: VMEM, outs),
            scratch_shapes=list(scratch),
            compiler_params=pltpu.CompilerParams(vmem_limit_bytes=grant),
            cost_estimate=cost,
            input_output_aliases=aliases,
        )(*ins)

    ids = jnp.stack([tx_id, box_id]).astype(jnp.int32)
    planes = matrix.reshape(2, samples, width)
    pieces = call(
        functools.partial(slice_kernel, group),
        (jax.ShapeDtypeStruct((2, piece, width), BF16),) * group,
        (ids, planes),
        [pltpu.SemaphoreType.DMA((group,))],
        [SMEM, pl.BlockSpec(memory_space=pl.ANY)],
        WHOLE,
    )
    order = sorted(range(2, group - 1), key=lambda o: (bin(o // 2).count("1"), o % 2, o))
    pieces = list(pieces)
    for other in order + [1]:
        pieces[other] = swap(pieces[other], 0, other)
    pieces[-1] = swap(pieces[-1], 0, group - 1)

    rows_up = -(-(each + 3) // 16) * 16
    held = lax.optimization_barrier((pieces[0], ids, counts, incident[:, 0, :], contrast_tangent, background))
    pieces[0] = held[0]

    def joined(left, right):
        shape = (2 * left.shape[0],) + left.shape[1:]
        return call(join_kernel, jax.ShapeDtypeStruct(shape, BF16), (left, right), grant=SMALL)

    packed = call(
        functools.partial(pack_kernel, tx_total),
        jax.ShapeDtypeStruct((1, rows_up, width), BF16),
        held[1:],
        specs=[SMEM, SMEM, VMEM, VMEM, VMEM],
        grant=SMALL,
    )
    for bit in [1] + tx_bits:
        packed = joined(packed, swap_member(packed, bit))
    packed = [packed] + [swap_member(packed, other) for other in range(2, group, 2)]
    cosine, sine_part = call(
        functools.partial(phase_kernel, group, samples),
        (jax.ShapeDtypeStruct((piece, group), F32),) * 2,
        (ids, centers),
        [pltpu.VMEM((group, piece), F32)],
        [SMEM, SMEM],
        SMALL,
    )

    rows_type = jax.ShapeDtypeStruct((2 * piece, group * width), BF16)
    flat_type = pltpu.VMEM((count, group * width), BF16)
    top_types = (
        jax.ShapeDtypeStruct((count, 2 * piece), F32),
        jax.ShapeDtypeStruct((count, 2 * piece), BF16),
    )
    even_type = jax.ShapeDtypeStruct((members // 2, each, width), BF16)
    part_types = (jax.ShapeDtypeStruct(even_type.shape, F32), even_type)
    whole_type = jax.ShapeDtypeStruct((members, each, width), F32)
    coef_type = jax.ShapeDtypeStruct((2, group // 2, width), F32)
    work = pl.CostEstimate(
        flops=2 * count * 2 * piece * group * width,
        bytes_accessed=2 * 2 * piece * group * width,
        transcendentals=0,
    )

    def other_half(send):
        return swap(send, 0, group) if halves == 2 else jnp.zeros_like(send)

    sum_bits = tx_bits + box_bits[1:]

    def summed(part, send):
        part = part + swap_member(send, 1).astype(F32)
        for bit in sum_bits[:-1]:
            arrived = swap_member(part.astype(BF16), bit)
            arrived = arrived.reshape(-1, 2, bit // 2, each, width)[:, ::-1]
            part = part + arrived.reshape(part.shape).astype(F32)
        return part, swap_member(part.astype(BF16), sum_bits[-1])

    def next_top(even):
        return call(
            functools.partial(top_kernel, group),
            top_types,
            (even, swap_member(even, 1), rows),
            [flat_type],
            cost=work,
        )

    rows, source_one, coefs, top, late = call(
        functools.partial(fill_kernel, group, tx_total, each),
        (rows_type, even_type, coef_type, top_types[0], jax.ShapeDtypeStruct((count, width), BF16)),
        (*pieces[:-1], cosine, sine_part, *packed),
        [pltpu.VMEM((count, (group - 1) * width), BF16)],
        cost=work,
    )
    rows, top, send = call(
        functools.partial(finish_kernel, group),
        (rows_type,) + top_types,
        (pieces[-1], cosine, sine_part, late, top, rows),
        aliases={5: 0},
    )
    back = functools.partial(back_kernel, group)
    source = functools.partial(source_kernel, group, sum_bits[-1] // 2)
    part, arrived = summed(*call(back, part_types, (top, other_half(send), rows)))
    source_two = call(
        functools.partial(source, False), even_type, (part, arrived, coefs, source_one)
    )
    top, send = next_top(source_two)
    part, send, kept = call(back, part_types + (whole_type,), (top, other_half(send), rows))
    part, arrived = summed(part, send)
    weighted = call(functools.partial(source, True), even_type, (part, arrived, coefs))
    top, send = next_top(weighted)
    product = call(
        functools.partial(last_kernel, group, tx_total, each),
        jax.ShapeDtypeStruct((group, width), F32),
        (top, other_half(send), rows, kept, *packed),
    )
    for bit in reversed(box_bits):
        product = product[:bit] + swap_member(product[bit:], bit)
    for bit in tx_bits:
        product = product + swap_member(product, bit)
    live = (jnp.arange(width // 2, dtype=jnp.int32)[None, :] < counts[:, None]).astype(F32)
    product = jnp.concatenate([live, live], -1) * product
    piece_width = width // tx_total
    return lax.dynamic_slice_in_dim(product, tx_id * piece_width, piece_width, 1)


def solution(mesh):
    placed = (
        P("box", "tx"),
        P("tx", "box", None),
        P("box", None),
        P("box"),
        P("box", None, None),
        P(),
    )
    return jax.shard_map(
        shards, mesh=mesh, in_specs=placed, out_specs=P("box", "tx"), check_vma=False
    )
```

profile of v0, /device:TPU:0, one launch (start us, length us, event | category | flops | bytes accessed | tf_op | source)
XLA Modules:
  0.0 121.4 jit_solution(10529589866601643524)
XLA Ops:
  0.6 3.7 %shard_map.64 = (bf16[2,512,128]{2,1,0:T(8,128)(2,1)}, bf16[2,512,128]{2,1,0:T(8,128)(2,1)}, bf16[2,512,128]{2,1,0:T(8,128)(2,1)}, bf16[2,512,128]{2,1,0:T(8,128...) custom-call(s32[2]{0:T(128)} %pad_add_fusion.ids_ref, ...), custom_call_target="tpu_custom_call" | custom-call | tf_op jit(solution)/shard_map/pallas_call | solution.py:230
  4.9 2.6 %collective-permute-start.2 = (bf16[2,512,128]{2,1,0:T(8,128)(2,1)}, bf16[2,512,128]{2,1,0:T(8,128)(2,1)S(1)}, u32[]{:S(2)}, u32[]{:S(2)}) collective-permute-start(bf16[2,512,128]{2,1,0:T(8,128)(2,1)} %get-tuple-element.44), channel_id=1, source_target_pairs={{0,2},{1,3},{2,0},{3,1},{4,6},{5,7},{6,4},{7,5},{8,10},{9,11},{10,... | collective-permute-start | bytes 786440 | tf_op jit(solution)/shard_map/ppermute | solution.py:224
  11.4 2.3 %collective-permute-done.8.right_ref = bf16[2,48,128]{2,1,0:T(8,128)(2,1)S(1)} collective-permute-done((bf16[2,48,128]{2,1,0:T(8,128)(2,1)S(1)}, bf16[2,48,128]{2,1,0:T(8,128)(2,1)S(1)}, u32[]{:S(2)}, u32[]{:S(2)}) %collective-permute-start.8) | collective-permute-done | bytes 24608 | tf_op jit(solution)/shard_map/ppermute | solution.py:224
  15.4 1.8 %collective-permute-start.9 = (bf16[4,48,128]{2,1,0:T(8,128)(2,1)S(1)}, bf16[4,48,128]{2,1,0:T(8,128)(2,1)S(1)}, u32[]{:S(2)}, u32[]{:S(2)}) collective-permute-start(bf16[4,48,128]{2,1,0:T(8,128)(2,1)S(1)} %shard_map.68.refs_9_.refs_0_), channel_id=1, source_target_pairs={{0,2},{1,3},{2,0},{3,1},{4,6},{5,7},{6,4},{7,5},{8,10},{9,11},{10,... | collective-permute-start | bytes 147464 | tf_op jit(solution)/shard_map/ppermute | solution.py:224
  20.9 2.4 %collective-permute-start.6 = (bf16[2,512,128]{2,1,0:T(8,128)(2,1)}, bf16[2,512,128]{2,1,0:T(8,128)(2,1)S(1)}, u32[]{:S(2)}, u32[]{:S(2)}) collective-permute-start(bf16[2,512,128]{2,1,0:T(8,128)(2,1)} %get-tuple-element.48), channel_id=1, source_target_pairs={{0,6},{1,7},{2,4},{3,5},{4,2},{5,3},{6,0},{7,1},{8,14},{9,15},{10,... | collective-permute-start | bytes 786440 | tf_op jit(solution)/shard_map/ppermute | solution.py:224
  24.7 2.0 %collective-permute-done.3.refs_3_ = bf16[2,512,128]{2,1,0:T(8,128)(2,1)S(1)} collective-permute-done((bf16[2,512,128]{2,1,0:T(8,128)(2,1)}, bf16[2,512,128]{2,1,0:T(8,128)(2,1)S(1)}, u32[]{:S(2)}, u32[]{:S(2)}) %collective-permute-start.3) | collective-permute-done | bytes 262176 | tf_op jit(solution)/shard_map/ppermute | solution.py:224
  26.8 2.0 %collective-permute-done.4.refs_4_ = bf16[2,512,128]{2,1,0:T(8,128)(2,1)S(1)} collective-permute-done((bf16[2,512,128]{2,1,0:T(8,128)(2,1)}, bf16[2,512,128]{2,1,0:T(8,128)(2,1)S(1)}, u32[]{:S(2)}, u32[]{:S(2)}) %collective-permute-start.4) | collective-permute-done | bytes 262176 | tf_op jit(solution)/shard_map/ppermute | solution.py:224
  28.8 4.2 %collective-permute-done.5.refs_5_ = bf16[2,512,128]{2,1,0:T(8,128)(2,1)S(1)} collective-permute-done((bf16[2,512,128]{2,1,0:T(8,128)(2,1)}, bf16[2,512,128]{2,1,0:T(8,128)(2,1)S(1)}, u32[]{:S(2)}, u32[]{:S(2)}) %collective-permute-start.5) | collective-permute-done | bytes 262176 | tf_op jit(solution)/shard_map/ppermute | solution.py:224
  33.0 8.0 %collective-permute-done.6.refs_6_ = bf16[2,512,128]{2,1,0:T(8,128)(2,1)S(1)} collective-permute-done((bf16[2,512,128]{2,1,0:T(8,128)(2,1)}, bf16[2,512,128]{2,1,0:T(8,128)(2,1)S(1)}, u32[]{:S(2)}, u32[]{:S(2)}) %collective-permute-start.6) | collective-permute-done | bytes 262176 | tf_op jit(solution)/shard_map/ppermute | solution.py:224
  41.9 1.7 %shard_map.69 = (bf16[1024,1024]{1,0:T(8,128)(2,1)S(1)}, bf16[8,32,128]{2,1,0:T(8,128)(2,1)S(1)}, f32[2,4,128]{2,1,0:T(4,128)S(1)}, f32[64,1024]{1,0:T(8,128)S(1)}, bf16[64,128]{1,0:T(8,128)(2,1)S(1)}) custom-call(bf16[2,512,128]{2,1,0:T(8,128)(2,1)S(1)} %copy-done, bf16[2,512,128]{2,1,0:T(8,128)(2,1)S(1)} %collective-permute-done.1.refs_1_, ...), custom_call_target="tpu_custom_call" | custom-call | flops 134217728 | bytes 2097152 | tf_op jit(solution)/shard_map/pallas_call | solution.py:230
  45.4 2.7 %collective-permute-start.12 = (bf16[64,1024]{1,0:T(8,128)(2,1)S(1)}, bf16[64,1024]{1,0:T(8,128)(2,1)S(1)}, u32[]{:S(2)}, u32[]{:S(2)}) collective-permute-start(bf16[64,1024]{1,0:T(8,128)(2,1)S(1)} %get-tuple-element.58), channel_id=1, source_target_pairs={{0,8},{1,9},{2,10},{3,11},{4,12},{5,13},{6,14},{7,15},{8,0},{9,1},... | collective-permute-start | bytes 393224 | tf_op jit(solution)/shard_map/ppermute | solution.py:224
  48.1 7.1 %collective-permute-done.12.other_ref = bf16[64,1024]{1,0:T(8,128)(2,1)S(1)} collective-permute-done((bf16[64,1024]{1,0:T(8,128)(2,1)S(1)}, bf16[64,1024]{1,0:T(8,128)(2,1)S(1)}, u32[]{:S(2)}, u32[]{:S(2)}) %collective-permute-start.12) | collective-permute-done | bytes 131104 | tf_op jit(solution)/shard_map/ppermute | solution.py:224
  58.6 2.8 %collective-permute-done.14 = bf16[8,32,128]{2,1,0:T(8,128)(2,1)S(1)} collective-permute-done((bf16[8,32,128]{2,1,0:T(8,128)(2,1)S(1)}, bf16[8,32,128]{2,1,0:T(8,128)(2,1)S(1)}, u32[]{:S(2)}, u32[]{:S(2)}) %collective-permute-start.14) | collective-permute-done | bytes 65568 | tf_op jit(solution)/shard_map/ppermute | solution.py:224
  62.0 3.7 %collective-permute-done.15 = bf16[8,32,128]{2,1,0:T(8,128)(2,1)S(1)} collective-permute-done((bf16[8,32,128]{2,1,0:T(8,128)(2,1)S(1)}, bf16[8,32,128]{2,1,0:T(8,128)(2,1)S(1)}, u32[]{:S(2)}, u32[]{:S(2)}) %collective-permute-start.15) | collective-permute-done | bytes 65568 | tf_op jit(solution)/shard_map/ppermute | solution.py:224
  66.5 3.6 %collective-permute-done.16.other_ref = bf16[8,32,128]{2,1,0:T(8,128)(2,1)S(1)} collective-permute-done((bf16[8,32,128]{2,1,0:T(8,128)(2,1)S(1)}, bf16[8,32,128]{2,1,0:T(8,128)(2,1)S(1)}, u32[]{:S(2)}, u32[]{:S(2)}) %collective-permute-start.16) | collective-permute-done | bytes 65568 | tf_op jit(solution)/shard_map/ppermute | solution.py:224
  72.3 2.1 %collective-permute-start.18 = (bf16[64,1024]{1,0:T(8,128)(2,1)S(1)}, bf16[64,1024]{1,0:T(8,128)(2,1)S(1)}, u32[]{:S(2)}, u32[]{:S(2)}) collective-permute-start(bf16[64,1024]{1,0:T(8,128)(2,1)S(1)} %get-tuple-element.65), channel_id=1, source_target_pairs={{0,8},{1,9},{2,10},{3,11},{4,12},{5,13},{6,14},{7,15},{8,0},{9,1},... | collective-permute-start | bytes 393224 | tf_op jit(solution)/shard_map/ppermute | solution.py:224
  74.4 7.2 %collective-permute-done.18.other_ref = bf16[64,1024]{1,0:T(8,128)(2,1)S(1)} collective-permute-done((bf16[64,1024]{1,0:T(8,128)(2,1)S(1)}, bf16[64,1024]{1,0:T(8,128)(2,1)S(1)}, u32[]{:S(2)}, u32[]{:S(2)}) %collective-permute-start.18) | collective-permute-done | bytes 131104 | tf_op jit(solution)/shard_map/ppermute | solution.py:224
  85.1 2.8 %collective-permute-done.20 = bf16[8,32,128]{2,1,0:T(8,128)(2,1)S(1)} collective-permute-done((bf16[8,32,128]{2,1,0:T(8,128)(2,1)S(1)}, bf16[8,32,128]{2,1,0:T(8,128)(2,1)S(1)}, u32[]{:S(2)}, u32[]{:S(2)}) %collective-permute-start.20) | collective-permute-done | bytes 65568 | tf_op jit(solution)/shard_map/ppermute | solution.py:224
  88.5 3.7 %collective-permute-done.21 = bf16[8,32,128]{2,1,0:T(8,128)(2,1)S(1)} collective-permute-done((bf16[8,32,128]{2,1,0:T(8,128)(2,1)S(1)}, bf16[8,32,128]{2,1,0:T(8,128)(2,1)S(1)}, u32[]{:S(2)}, u32[]{:S(2)}) %collective-permute-start.21) | collective-permute-done | bytes 65568 | tf_op jit(solution)/shard_map/ppermute | solution.py:224
  92.5 4.1 %collective-permute-done.22.other_ref = bf16[8,32,128]{2,1,0:T(8,128)(2,1)S(1)} collective-permute-done((bf16[8,32,128]{2,1,0:T(8,128)(2,1)S(1)}, bf16[8,32,128]{2,1,0:T(8,128)(2,1)S(1)}, u32[]{:S(2)}, u32[]{:S(2)}) %collective-permute-start.22) | collective-permute-done | bytes 65568 | tf_op jit(solution)/shard_map/ppermute | solution.py:224
  100.3 7.8 %collective-permute-done.24.other_ref = bf16[64,1024]{1,0:T(8,128)(2,1)S(1)} collective-permute-done((bf16[64,1024]{1,0:T(8,128)(2,1)S(1)}, bf16[64,1024]{1,0:T(8,128)(2,1)S(1)}, u32[]{:S(2)}, u32[]{:S(2)}) %collective-permute-start.24) | collective-permute-done | bytes 131104 | tf_op jit(solution)/shard_map/ppermute | solution.py:224
  108.9 3.6 %collective-permute-done.25 = f32[4,128]{1,0:T(4,128)S(1)} collective-permute-done((f32[4,128]{1,0:T(4,128)S(1)}, f32[4,128]{1,0:T(4,128)S(1)}, u32[]{:S(2)}, u32[]{:S(2)}) %collective-permute-start.25) | collective-permute-done | bytes 2080 | tf_op jit(solution)/shard_map/ppermute | solution.py:224
  113.0 3.0 %collective-permute-done.26 = f32[2,128]{1,0:T(2,128)S(1)} collective-permute-done((f32[2,128]{1,0:T(2,128)S(1)}, f32[2,128]{1,0:T(2,128)S(1)}, u32[]{:S(2)}, u32[]{:S(2)}) %collective-permute-start.26) | collective-permute-done | bytes 1056 | tf_op jit(solution)/shard_map/ppermute | solution.py:224
  118.7 2.1 %collective-permute-done.28 = f32[1,128]{1,0:T(1,128)S(1)} collective-permute-done((f32[1,128]{1,0:T(1,128)S(1)}, f32[1,128]{1,0:T(1,128)S(1)}, u32[]{:S(2)}, u32[]{:S(2)}) %collective-permute-start.28) | collective-permute-done | bytes 544 | tf_op jit(solution)/shard_map/ppermute | solution.py:224
  (80 shorter events, 33.4 us)
Async XLA Ops:
  4.3 16.6 %collective-permute-start.1 = (bf16[2,512,128]{2,1,0:T(8,128)(2,1)}, bf16[2,512,128]{2,1,0:T(8,128)(2,1)S(1)}, u32[]{:S(2)}, u32[]{:S(2)}) collective-permute-start(bf16[2,512,128]{2,1,0:T(8,128)(2,1)} %get-tuple-element.43), channel_id=1, source_target_pairs={{0,1},{1,0},{2,3},{3,2},{4,5},{5,4},{6,7},{7,6},{8,9},{9,8},{10,11... | collective-permute-start | bytes 786440 | tf_op jit(solution)/shard_map/ppermute | solution.py:224
  4.9 18.4 %collective-permute-start.2 = (bf16[2,512,128]{2,1,0:T(8,128)(2,1)}, bf16[2,512,128]{2,1,0:T(8,128)(2,1)S(1)}, u32[]{:S(2)}, u32[]{:S(2)}) collective-permute-start(bf16[2,512,128]{2,1,0:T(8,128)(2,1)} %get-tuple-element.44), channel_id=1, source_target_pairs={{0,2},{1,3},{2,0},{3,1},{4,6},{5,7},{6,4},{7,5},{8,10},{9,11},{10,... | collective-permute-start | bytes 786440 | tf_op jit(solution)/shard_map/ppermute | solution.py:224
  9.9 3.8 %collective-permute-start.8 = (bf16[2,48,128]{2,1,0:T(8,128)(2,1)S(1)}, bf16[2,48,128]{2,1,0:T(8,128)(2,1)S(1)}, u32[]{:S(2)}, u32[]{:S(2)}) collective-permute-start(bf16[2,48,128]{2,1,0:T(8,128)(2,1)S(1)} %shard_map.67.left_ref), channel_id=1, source_target_pairs={{0,16},{1,17},{2,18},{3,19},{4,20},{5,21},{6,22},{7,23},{8,24},{9,... | collective-permute-start | bytes 73736 | tf_op jit(solution)/shard_map/ppermute | solution.py:224
  13.8 5.2 %collective-permute-start.11 = (bf16[4,48,128]{2,1,0:T(8,128)(2,1)S(1)}, bf16[4,48,128]{2,1,0:T(8,128)(2,1)S(1)}, u32[]{:S(2)}, u32[]{:S(2)}) collective-permute-start(bf16[4,48,128]{2,1,0:T(8,128)(2,1)S(1)} %shard_map.68.refs_9_.refs_0_), channel_id=1, source_target_pairs={{0,6},{1,7},{2,4},{3,5},{4,2},{5,3},{6,0},{7,1},{8,14},{9,15},{10,... | collective-permute-start | bytes 147464 | tf_op jit(solution)/shard_map/ppermute | solution.py:224
  15.3 4.1 %collective-permute-start.10 = (bf16[4,48,128]{2,1,0:T(8,128)(2,1)S(1)}, bf16[4,48,128]{2,1,0:T(8,128)(2,1)S(1)}, u32[]{:S(2)}, u32[]{:S(2)}) collective-permute-start(bf16[4,48,128]{2,1,0:T(8,128)(2,1)S(1)} %shard_map.68.refs_9_.refs_0_), channel_id=1, source_target_pairs={{0,4},{1,5},{2,6},{3,7},{4,0},{5,1},{6,2},{7,3},{8,12},{9,13},{10,... | collective-permute-start | bytes 147464 | tf_op jit(solution)/shard_map/ppermute | solution.py:224
  15.4 4.9 %collective-permute-start.9 = (bf16[4,48,128]{2,1,0:T(8,128)(2,1)S(1)}, bf16[4,48,128]{2,1,0:T(8,128)(2,1)S(1)}, u32[]{:S(2)}, u32[]{:S(2)}) collective-permute-start(bf16[4,48,128]{2,1,0:T(8,128)(2,1)S(1)} %shard_map.68.refs_9_.refs_0_), channel_id=1, source_target_pairs={{0,2},{1,3},{2,0},{3,1},{4,6},{5,7},{6,4},{7,5},{8,10},{9,11},{10,... | collective-permute-start | bytes 147464 | tf_op jit(solution)/shard_map/ppermute | solution.py:224
  18.9 7.8 %collective-permute-start.3 = (bf16[2,512,128]{2,1,0:T(8,128)(2,1)}, bf16[2,512,128]{2,1,0:T(8,128)(2,1)S(1)}, u32[]{:S(2)}, u32[]{:S(2)}) collective-permute-start(bf16[2,512,128]{2,1,0:T(8,128)(2,1)} %get-tuple-element.45), channel_id=1, source_target_pairs={{0,3},{1,2},{2,1},{3,0},{4,7},{5,6},{6,5},{7,4},{8,11},{9,10},{10,... | collective-permute-start | bytes 786440 | tf_op jit(solution)/shard_map/ppermute | solution.py:224
  19.4 9.4 %collective-permute-start.4 = (bf16[2,512,128]{2,1,0:T(8,128)(2,1)}, bf16[2,512,128]{2,1,0:T(8,128)(2,1)S(1)}, u32[]{:S(2)}, u32[]{:S(2)}) collective-permute-start(bf16[2,512,128]{2,1,0:T(8,128)(2,1)} %get-tuple-element.46), channel_id=1, source_target_pairs={{0,4},{1,5},{2,6},{3,7},{4,0},{5,1},{6,2},{7,3},{8,12},{9,13},{10,... | collective-permute-start | bytes 786440 | tf_op jit(solution)/shard_map/ppermute | solution.py:224
  20.4 12.6 %collective-permute-start.5 = (bf16[2,512,128]{2,1,0:T(8,128)(2,1)}, bf16[2,512,128]{2,1,0:T(8,128)(2,1)S(1)}, u32[]{:S(2)}, u32[]{:S(2)}) collective-permute-start(bf16[2,512,128]{2,1,0:T(8,128)(2,1)} %get-tuple-element.47), channel_id=1, source_target_pairs={{0,5},{1,4},{2,7},{3,6},{4,1},{5,0},{6,3},{7,2},{8,13},{9,12},{10,... | collective-permute-start | bytes 786440 | tf_op jit(solution)/shard_map/ppermute | solution.py:224
  20.9 20.1 %collective-permute-start.6 = (bf16[2,512,128]{2,1,0:T(8,128)(2,1)}, bf16[2,512,128]{2,1,0:T(8,128)(2,1)S(1)}, u32[]{:S(2)}, u32[]{:S(2)}) collective-permute-start(bf16[2,512,128]{2,1,0:T(8,128)(2,1)} %get-tuple-element.48), channel_id=1, source_target_pairs={{0,6},{1,7},{2,4},{3,5},{4,2},{5,3},{6,0},{7,1},{8,14},{9,15},{10,... | collective-permute-start | bytes 786440 | tf_op jit(solution)/shard_map/ppermute | solution.py:224
  23.3 21.7 %collective-permute-start = (bf16[2,512,128]{2,1,0:T(8,128)(2,1)}, bf16[2,512,128]{2,1,0:T(8,128)(2,1)S(1)}, u32[]{:S(2)}, u32[]{:S(2)}) collective-permute-start(bf16[2,512,128]{2,1,0:T(8,128)(2,1)} %get-tuple-element.38), channel_id=1, source_target_pairs={{0,7},{1,6},{2,5},{3,4},{4,3},{5,2},{6,1},{7,0},{8,15},{9,14},{10,... | collective-permute-start | bytes 786440 | tf_op jit(solution)/shard_map/ppermute | solution.py:224
  45.4 9.8 %collective-permute-start.12 = (bf16[64,1024]{1,0:T(8,128)(2,1)S(1)}, bf16[64,1024]{1,0:T(8,128)(2,1)S(1)}, u32[]{:S(2)}, u32[]{:S(2)}) collective-permute-start(bf16[64,1024]{1,0:T(8,128)(2,1)S(1)} %get-tuple-element.58), channel_id=1, source_target_pairs={{0,8},{1,9},{2,10},{3,11},{4,12},{5,13},{6,14},{7,15},{8,0},{9,1},... | collective-permute-start | bytes 393224 | tf_op jit(solution)/shard_map/ppermute | solution.py:224
  55.7 1.3 %collective-permute-start.13 = (bf16[8,32,128]{2,1,0:T(8,128)(2,1)S(1)}, bf16[8,32,128]{2,1,0:T(8,128)(2,1)S(1)}, u32[]{:S(2)}, u32[]{:S(2)}) collective-permute-start(bf16[8,32,128]{2,1,0:T(8,128)(2,1)S(1)} %get-tuple-element.61), channel_id=1, source_target_pairs={{0,1},{1,0},{2,3},{3,2},{4,5},{5,4},{6,7},{7,6},{8,9},{9,8},{10,11... | collective-permute-start | bytes 196616 | tf_op jit(solution)/shard_map/ppermute | solution.py:224
  57.1 4.3 %collective-permute-start.14 = (bf16[8,32,128]{2,1,0:T(8,128)(2,1)S(1)}, bf16[8,32,128]{2,1,0:T(8,128)(2,1)S(1)}, u32[]{:S(2)}, u32[]{:S(2)}) collective-permute-start(bf16[8,32,128]{2,1,0:T(8,128)(2,1)S(1)} %fusion), channel_id=1, source_target_pairs={{0,16},{1,17},{2,18},{3,19},{4,20},{5,21},{6,22},{7,23},{8,24},{9,... | collective-permute-start | bytes 196616 | tf_op jit(solution)/shard_map/ppermute | solution.py:224
  61.4 4.3 %collective-permute-start.15 = (bf16[8,32,128]{2,1,0:T(8,128)(2,1)S(1)}, bf16[8,32,128]{2,1,0:T(8,128)(2,1)S(1)}, u32[]{:S(2)}, u32[]{:S(2)}) collective-permute-start(bf16[8,32,128]{2,1,0:T(8,128)(2,1)S(1)} %fusion.2), channel_id=1, source_target_pairs={{0,2},{1,3},{2,0},{3,1},{4,6},{5,7},{6,4},{7,5},{8,10},{9,11},{10,... | collective-permute-start | bytes 196616 | tf_op jit(solution)/shard_map/ppermute | solution.py:224
  65.8 4.3 %collective-permute-start.16 = (bf16[8,32,128]{2,1,0:T(8,128)(2,1)S(1)}, bf16[8,32,128]{2,1,0:T(8,128)(2,1)S(1)}, u32[]{:S(2)}, u32[]{:S(2)}) collective-permute-start(bf16[8,32,128]{2,1,0:T(8,128)(2,1)S(1)} %get-tuple-element.73), channel_id=1, source_target_pairs={{0,4},{1,5},{2,6},{3,7},{4,0},{5,1},{6,2},{7,3},{8,12},{9,13},{10,... | collective-permute-start | bytes 196616 | tf_op jit(solution)/shard_map/ppermute | solution.py:224
  72.3 9.3 %collective-permute-start.18 = (bf16[64,1024]{1,0:T(8,128)(2,1)S(1)}, bf16[64,1024]{1,0:T(8,128)(2,1)S(1)}, u32[]{:S(2)}, u32[]{:S(2)}) collective-permute-start(bf16[64,1024]{1,0:T(8,128)(2,1)S(1)} %get-tuple-element.65), channel_id=1, source_target_pairs={{0,8},{1,9},{2,10},{3,11},{4,12},{5,13},{6,14},{7,15},{8,0},{9,1},... | collective-permute-start | bytes 393224 | tf_op jit(solution)/shard_map/ppermute | solution.py:224
  83.5 4.3 %collective-permute-start.20 = (bf16[8,32,128]{2,1,0:T(8,128)(2,1)S(1)}, bf16[8,32,128]{2,1,0:T(8,128)(2,1)S(1)}, u32[]{:S(2)}, u32[]{:S(2)}) collective-permute-start(bf16[8,32,128]{2,1,0:T(8,128)(2,1)S(1)} %fusion.1), channel_id=1, source_target_pairs={{0,16},{1,17},{2,18},{3,19},{4,20},{5,21},{6,22},{7,23},{8,24},{9,... | collective-permute-start | bytes 196616 | tf_op jit(solution)/shard_map/ppermute | solution.py:224
  87.9 4.3 %collective-permute-start.21 = (bf16[8,32,128]{2,1,0:T(8,128)(2,1)S(1)}, bf16[8,32,128]{2,1,0:T(8,128)(2,1)S(1)}, u32[]{:S(2)}, u32[]{:S(2)}) collective-permute-start(bf16[8,32,128]{2,1,0:T(8,128)(2,1)S(1)} %fusion.3), channel_id=1, source_target_pairs={{0,2},{1,3},{2,0},{3,1},{4,6},{5,7},{6,4},{7,5},{8,10},{9,11},{10,... | collective-permute-start | bytes 196616 | tf_op jit(solution)/shard_map/ppermute | solution.py:224
  92.3 4.3 %collective-permute-start.22 = (bf16[8,32,128]{2,1,0:T(8,128)(2,1)S(1)}, bf16[8,32,128]{2,1,0:T(8,128)(2,1)S(1)}, u32[]{:S(2)}, u32[]{:S(2)}) collective-permute-start(bf16[8,32,128]{2,1,0:T(8,128)(2,1)S(1)} %get-tuple-element.71), channel_id=1, source_target_pairs={{0,4},{1,5},{2,6},{3,7},{4,0},{5,1},{6,2},{7,3},{8,12},{9,13},{10,... | collective-permute-start | bytes 196616 | tf_op jit(solution)/shard_map/ppermute | solution.py:224
  98.8 9.3 %collective-permute-start.24 = (bf16[64,1024]{1,0:T(8,128)(2,1)S(1)}, bf16[64,1024]{1,0:T(8,128)(2,1)S(1)}, u32[]{:S(2)}, u32[]{:S(2)}) collective-permute-start(bf16[64,1024]{1,0:T(8,128)(2,1)S(1)} %get-tuple-element.69), channel_id=1, source_target_pairs={{0,8},{1,9},{2,10},{3,11},{4,12},{5,13},{6,14},{7,15},{8,0},{9,1},... | collective-permute-start | bytes 393224 | tf_op jit(solution)/shard_map/ppermute | solution.py:224
  108.8 3.7 %collective-permute-start.25 = (f32[4,128]{1,0:T(4,128)S(1)}, f32[4,128]{1,0:T(4,128)S(1)}, u32[]{:S(2)}, u32[]{:S(2)}) collective-permute-start(f32[4,128]{1,0:T(4,128)S(1)} %slice.19), channel_id=1, source_target_pairs={{0,4},{1,5},{2,6},{3,7},{4,0},{5,1},{6,2},{7,3},{8,12},{9,13},{10,... | collective-permute-start | bytes 6152 | tf_op jit(solution)/shard_map/ppermute | solution.py:224
  112.5 3.6 %collective-permute-start.26 = (f32[2,128]{1,0:T(2,128)S(1)}, f32[2,128]{1,0:T(2,128)S(1)}, u32[]{:S(2)}, u32[]{:S(2)}) collective-permute-start(f32[2,128]{1,0:T(2,128)S(1)} %slice.21), channel_id=1, source_target_pairs={{0,2},{1,3},{2,0},{3,1},{4,6},{5,7},{6,4},{7,5},{8,10},{9,11},{10,... | collective-permute-start | bytes 3080 | tf_op jit(solution)/shard_map/ppermute | solution.py:224
  117.2 3.6 %collective-permute-start.28 = (f32[1,128]{1,0:T(1,128)S(1)}, f32[1,128]{1,0:T(1,128)S(1)}, u32[]{:S(2)}, u32[]{:S(2)}) collective-permute-start(f32[1,128]{1,0:T(1,128)S(1)} %slice_add_fusion.2), channel_id=1, source_target_pairs={{0,16},{1,17},{2,18},{3,19},{4,20},{5,21},{6,22},{7,23},{8,24},{9,... | collective-permute-start | bytes 1544 | tf_op jit(solution)/shard_map/ppermute | solution.py:224
  (11 other events, 60.7 us)
where the time goes:
time: 122 us; the launch traced here: 121 us
  waiting for transfers between devices  80.7 us (66%)
  starting transfers between devices  26.7 us (22%)
  Pallas kernels  10.8 us (9%)
  local copies, waits for them, and re-layouts  1.6 us (1%)
    ppermute x29, waiting for transfers between devices, swap(): return lax.ppermute(value, ('tx', 'box'), pairs)  80.7 us
    ppermute x29, starting transfers between devices, swap(): return lax.ppermute(value, ('tx', 'box'), pairs)  26.7 us
    pallas_call x14, Pallas kernels, call(): pl.pallas_call(kernel, out_shape=outs, in_specs=specs or [VMEM] * len(ins...  10.8 us
  transfers between devices with their start and end apart: 29, of which 26 were waited for; matrix products, arithmetic and copies ran while one was open for 0% of the time, Pallas kernels for 3%

commit v1 on v0

--- a/solution.py
+++ b/solution.py
@@ -14,7 +14,7 @@
 SMEM = pl.BlockSpec(memory_space=pltpu.SMEM)
 GRANT = 12 << 20
 SMALL = 2 << 20
-WHOLE = 60 << 20
+WHOLE = 50 << 20
 CONTRACT_LAST = (((1,), (1,)), ((), ()))
 
 
@@ -27,12 +27,12 @@
     return pltpu.roll(values, values.shape[-1] // 2, axis=values.ndim - 1)
 
 
-def slice_kernel(total, ids_ref, planes_ref, *refs):
+def slice_kernel(total, planes_ref, *refs):
     outs, sems = refs[:total], refs[total]
     size = outs[0].shape[1]
     copies = []
     for other in reversed(range(total)):
-        chunk = ids_ref[0] * total + ((ids_ref[1] ^ other) & (total - 1))
+        chunk = lax.axis_index("tx") * total + ((lax.axis_index("box") ^ other) & (total - 1))
         source = planes_ref.at[:, pl.ds(pl.multiple_of(chunk * size, size), size), :]
         copies.append(pltpu.make_async_copy(source, outs[other], sems.at[other]))
     for copy in copies:
@@ -41,14 +41,14 @@
         copy.wait()
 
 
-def pack_kernel(tx_total, ids_ref, counts_ref, incident_ref, tangent_ref, backdrop_ref, out_ref):
+def pack_kernel(tx_total, counts_ref, incident_ref, tangent_ref, backdrop_ref, out_ref):
     each, width = incident_ref.shape
     out_ref[0, :each, :] = incident_ref[...]
     shape = (out_ref.shape[1] - each, width)
     row = lax.broadcasted_iota(jnp.int32, shape, 0)
     lane = lax.broadcasted_iota(jnp.int32, shape, 1)
     tangent = jnp.concatenate([tangent_ref[...].astype(F32)] * tx_total, axis=-1)
-    first = ids_ref[0] * (width // tx_total)
+    first = lax.axis_index("tx") * (width // tx_total)
     mine = (lane >= first) & (lane < first + width // tx_total)
     half = width // 2
     slot = jnp.where(lane < half, lane, lane - half)
@@ -64,9 +64,10 @@
     out_ref[at:] = right_ref[...]
 
 
-def phase_kernel(group, total, ids_ref, centers_ref, cos_ref, sin_ref, phase_ref):
+def phase_kernel(group, total, centers_ref, cos_ref, sin_ref, phase_ref):
     size = cos_ref.shape[0]
-    chunk = ids_ref[0] * group + (ids_ref[1] & (group - 1))
+    me = lax.axis_index("box")
+    chunk = lax.axis_index("tx") * group + (me & (group - 1))
     sample_ids = chunk * size + lax.broadcasted_iota(jnp.int32, (1, size), 1)
     height = 1.0 - (2.0 * sample_ids.astype(F32) + 1.0) / total
     radial = jnp.sqrt(1.0 - height * height)
@@ -74,7 +75,7 @@
     azimuth = 2.0 * jnp.pi / 4181.0 * turn_ids.astype(F32)
     along_x, along_y = radial * jnp.cos(azimuth), radial * jnp.sin(azimuth)
     for j in range(group):
-        box = ids_ref[1] ^ j
+        box = me ^ j
         phase_ref[j : j + 1] = jnp.pi * (
             centers_ref[0, box] * along_x + centers_ref[1, box] * along_y + centers_ref[2, box] * height
         )
@@ -203,7 +204,7 @@
 
 def shards(contrast_tangent, incident, background, counts, box_mats, centers):
     tx_total, box_total = lax.axis_size("tx"), lax.axis_size("box")
-    tx_id, box_id = lax.axis_index("tx"), lax.axis_index("box")
+    tx_id = lax.axis_index("tx")
     group = max(box_total // 2, 1)
     halves = box_total // group
     members = tx_total * group
@@ -238,14 +239,13 @@
             input_output_aliases=aliases,
         )(*ins)
 
-    ids = jnp.stack([tx_id, box_id]).astype(jnp.int32)
     planes = matrix.reshape(2, samples, width)
     pieces = call(
         functools.partial(slice_kernel, group),
         (jax.ShapeDtypeStruct((2, piece, width), BF16),) * group,
-        (ids, planes),
+        (planes,),
         [pltpu.SemaphoreType.DMA((group,))],
-        [SMEM, pl.BlockSpec(memory_space=pl.ANY)],
+        [pl.BlockSpec(memory_space=pl.ANY)],
         WHOLE,
     )
     order = sorted(range(2, group - 1), key=lambda o: (bin(o // 2).count("1"), o % 2, o))
@@ -255,7 +255,7 @@
     pieces[-1] = swap(pieces[-1], 0, group - 1)
 
     rows_up = -(-(each + 3) // 16) * 16
-    held = lax.optimization_barrier((pieces[0], ids, counts, incident[:, 0, :], contrast_tangent, background))
+    held = lax.optimization_barrier((pieces[0], counts, incident[:, 0, :], contrast_tangent, background))
     pieces[0] = held[0]
 
     def joined(left, right):
@@ -266,7 +266,7 @@
         functools.partial(pack_kernel, tx_total),
         jax.ShapeDtypeStruct((1, rows_up, width), BF16),
         held[1:],
-        specs=[SMEM, SMEM, VMEM, VMEM, VMEM],
+        specs=[SMEM, VMEM, VMEM, VMEM],
         grant=SMALL,
     )
     for bit in [1] + tx_bits:
@@ -275,9 +275,9 @@
     cosine, sine_part = call(
         functools.partial(phase_kernel, group, samples),
         (jax.ShapeDtypeStruct((piece, group), F32),) * 2,
-        (ids, centers),
+        (centers,),
         [pltpu.VMEM((group, piece), F32)],
-        [SMEM, SMEM],
+        [SMEM],
         SMALL,
     )
 

time: 122 us -> 116 us (0.951)
  waiting for transfers between devices: 80.7 us -> 75.4 us
  starting transfers between devices: 26.7 us -> 30.7 us
  Pallas kernels: 10.8 us -> 8.19 us
    ppermute x29, waiting for transfers between devices: 80.7 us -> 75.4 us  [swap(): return lax.ppermute(value, ('tx', 'box'), pairs)]
    ppermute x29, starting transfers between devices: 26.7 us -> 30.7 us  [swap(): return lax.ppermute(value, ('tx', 'box'), pairs)]
    pallas_call x14, Pallas kernels: 10.8 us -> 8.19 us  [call(): pl.pallas_call(kernel, out_shape=outs, in_specs=specs or [VMEM] * len(ins...]
  transfers between devices with their start and end apart: 29 -> 29, of which waited for: 26 -> 25; matrix products, arithmetic and copies ran while one was open for 0% -> 0% of each run, Pallas kernels for 3% -> 2%
where the time goes in v1:
time: 116 us
  waiting for transfers between devices  75.4 us (65%)
  starting transfers between devices  30.7 us (26%)
  Pallas kernels  8.19 us (7%)
    ppermute x29, waiting for transfers between devices, swap(): return lax.ppermute(value, ('tx', 'box'), pairs)  75.4 us
    ppermute x29, starting transfers between devices, swap(): return lax.ppermute(value, ('tx', 'box'), pairs)  30.7 us
    pallas_call x14, Pallas kernels, call(): pl.pallas_call(kernel, out_shape=outs, in_specs=specs or [VMEM] * len(ins...  8.19 us
  transfers between devices with their start and end apart: 29, of which 25 were waited for; matrix products, arithmetic and copies ran while one was open for 0% of the time, Pallas kernels for 2%

profile of v1, /device:TPU:0, one launch (start us, length us, event | category | flops | bytes accessed | tf_op | source)
XLA Modules:
  0.0 116.1 jit_solution(13526759448080832226)
XLA Ops:
  2.2 2.6 %collective-permute-start.2 = (bf16[2,512,128]{2,1,0:T(8,128)(2,1)S(1)}, bf16[2,512,128]{2,1,0:T(8,128)(2,1)S(1)}, u32[]{:S(2)}, u32[]{:S(2)}) collective-permute-start(bf16[2,512,128]{2,1,0:T(8,128)(2,1)S(1)} %get-tuple-element.43), channel_id=1, source_target_pairs={{0,2},{1,3},{2,0},{3,1},{4,6},{5,7},{6,4},{7,5},{8,10},{9,11},{10,... | collective-permute-start | bytes 786440 | tf_op jit(solution)/shard_map/ppermute | solution.py:225
  8.2 2.3 %collective-permute-done.8.right_ref = bf16[2,48,128]{2,1,0:T(8,128)(2,1)S(1)} collective-permute-done((bf16[2,48,128]{2,1,0:T(8,128)(2,1)S(1)}, bf16[2,48,128]{2,1,0:T(8,128)(2,1)S(1)}, u32[]{:S(2)}, u32[]{:S(2)}) %collective-permute-start.8) | collective-permute-done | bytes 24608 | tf_op jit(solution)/shard_map/ppermute | solution.py:225
  12.2 1.9 %collective-permute-start.9 = (bf16[4,48,128]{2,1,0:T(8,128)(2,1)S(1)}, bf16[4,48,128]{2,1,0:T(8,128)(2,1)S(1)}, u32[]{:S(2)}, u32[]{:S(2)}) collective-permute-start(bf16[4,48,128]{2,1,0:T(8,128)(2,1)S(1)} %shard_map.68.refs_9_.refs_0_), channel_id=1, source_target_pairs={{0,2},{1,3},{2,0},{3,1},{4,6},{5,7},{6,4},{7,5},{8,10},{9,11},{10,... | collective-permute-start | bytes 147464 | tf_op jit(solution)/shard_map/ppermute | solution.py:225
  14.8 2.5 %collective-permute-done.11.refs_12_.refs_3_ = bf16[4,48,128]{2,1,0:T(8,128)(2,1)S(1)} collective-permute-done((bf16[4,48,128]{2,1,0:T(8,128)(2,1)S(1)}, bf16[4,48,128]{2,1,0:T(8,128)(2,1)S(1)}, u32[]{:S(2)}, u32[]{:S(2)}) %collective-permute-start.11) | collective-permute-done | bytes 49184 | tf_op jit(solution)/shard_map/ppermute | solution.py:225
  19.2 2.4 %collective-permute-start = (bf16[2,512,128]{2,1,0:T(8,128)(2,1)S(1)}, bf16[2,512,128]{2,1,0:T(8,128)(2,1)S(1)}, u32[]{:S(2)}, u32[]{:S(2)}) collective-permute-start(bf16[2,512,128]{2,1,0:T(8,128)(2,1)S(1)} %get-tuple-element.37), channel_id=1, source_target_pairs={{0,7},{1,6},{2,5},{3,4},{4,3},{5,2},{6,1},{7,0},{8,15},{9,14},{10,... | collective-permute-start | bytes 786440 | tf_op jit(solution)/shard_map/ppermute | solution.py:225
  22.6 3.8 %collective-permute-done.4.refs_4_ = bf16[2,512,128]{2,1,0:T(8,128)(2,1)S(1)} collective-permute-done((bf16[2,512,128]{2,1,0:T(8,128)(2,1)S(1)}, bf16[2,512,128]{2,1,0:T(8,128)(2,1)S(1)}, u32[]{:S(2)}, u32[]{:S(2)}) %collective-permute-start.4) | collective-permute-done | bytes 262176 | tf_op jit(solution)/shard_map/ppermute | solution.py:225
  26.4 3.5 %collective-permute-done.5.refs_5_ = bf16[2,512,128]{2,1,0:T(8,128)(2,1)S(1)} collective-permute-done((bf16[2,512,128]{2,1,0:T(8,128)(2,1)S(1)}, bf16[2,512,128]{2,1,0:T(8,128)(2,1)S(1)}, u32[]{:S(2)}, u32[]{:S(2)}) %collective-permute-start.5) | collective-permute-done | bytes 262176 | tf_op jit(solution)/shard_map/ppermute | solution.py:225
  29.9 7.6 %collective-permute-done.6.refs_6_ = bf16[2,512,128]{2,1,0:T(8,128)(2,1)S(1)} collective-permute-done((bf16[2,512,128]{2,1,0:T(8,128)(2,1)S(1)}, bf16[2,512,128]{2,1,0:T(8,128)(2,1)S(1)}, u32[]{:S(2)}, u32[]{:S(2)}) %collective-permute-start.6) | collective-permute-done | bytes 262176 | tf_op jit(solution)/shard_map/ppermute | solution.py:225
  37.5 1.7 %shard_map.69 = (bf16[1024,1024]{1,0:T(8,128)(2,1)S(1)}, bf16[8,32,128]{2,1,0:T(8,128)(2,1)S(1)}, f32[2,4,128]{2,1,0:T(4,128)S(1)}, f32[64,1024]{1,0:T(8,128)S(1)}, bf16[64,128]{1,0:T(8,128)(2,1)S(1)}) custom-call(bf16[2,512,128]{2,1,0:T(8,128)(2,1)S(1)} %get-tuple-element.41.refs_0_, bf16[2,512,128]{2,1,0:T(8,128)(2,1)S(1)} %collective-permute-done.1.refs_1_, ...), custom_call_target="tpu_custom_call" | custom-call | flops 134217728 | bytes 2097152 | tf_op jit(solution)/shard_map/pallas_call | solution.py:231
  40.2 2.7 %collective-permute-start.12 = (bf16[64,1024]{1,0:T(8,128)(2,1)S(1)}, bf16[64,1024]{1,0:T(8,128)(2,1)S(1)}, u32[]{:S(2)}, u32[]{:S(2)}) collective-permute-start(bf16[64,1024]{1,0:T(8,128)(2,1)S(1)} %get-tuple-element.56), channel_id=1, source_target_pairs={{0,8},{1,9},{2,10},{3,11},{4,12},{5,13},{6,14},{7,15},{8,0},{9,1},... | collective-permute-start | bytes 393224 | tf_op jit(solution)/shard_map/ppermute | solution.py:225
  42.8 6.9 %collective-permute-done.12.other_ref = bf16[64,1024]{1,0:T(8,128)(2,1)S(1)} collective-permute-done((bf16[64,1024]{1,0:T(8,128)(2,1)S(1)}, bf16[64,1024]{1,0:T(8,128)(2,1)S(1)}, u32[]{:S(2)}, u32[]{:S(2)}) %collective-permute-start.12) | collective-permute-done | bytes 131104 | tf_op jit(solution)/shard_map/ppermute | solution.py:225
  53.1 2.9 %collective-permute-done.14 = bf16[8,32,128]{2,1,0:T(8,128)(2,1)S(1)} collective-permute-done((bf16[8,32,128]{2,1,0:T(8,128)(2,1)S(1)}, bf16[8,32,128]{2,1,0:T(8,128)(2,1)S(1)}, u32[]{:S(2)}, u32[]{:S(2)}) %collective-permute-start.14) | collective-permute-done | bytes 65568 | tf_op jit(solution)/shard_map/ppermute | solution.py:225
  57.5 2.9 %collective-permute-done.15 = bf16[8,32,128]{2,1,0:T(8,128)(2,1)S(1)} collective-permute-done((bf16[8,32,128]{2,1,0:T(8,128)(2,1)S(1)}, bf16[8,32,128]{2,1,0:T(8,128)(2,1)S(1)}, u32[]{:S(2)}, u32[]{:S(2)}) %collective-permute-start.15) | collective-permute-done | bytes 65568 | tf_op jit(solution)/shard_map/ppermute | solution.py:225
  61.6 3.1 %collective-permute-done.16.other_ref = bf16[8,32,128]{2,1,0:T(8,128)(2,1)S(1)} collective-permute-done((bf16[8,32,128]{2,1,0:T(8,128)(2,1)S(1)}, bf16[8,32,128]{2,1,0:T(8,128)(2,1)S(1)}, u32[]{:S(2)}, u32[]{:S(2)}) %collective-permute-start.16) | collective-permute-done | bytes 65568 | tf_op jit(solution)/shard_map/ppermute | solution.py:225
  67.0 2.5 %collective-permute-start.18 = (bf16[64,1024]{1,0:T(8,128)(2,1)S(1)}, bf16[64,1024]{1,0:T(8,128)(2,1)S(1)}, u32[]{:S(2)}, u32[]{:S(2)}) collective-permute-start(bf16[64,1024]{1,0:T(8,128)(2,1)S(1)} %get-tuple-element.63), channel_id=1, source_target_pairs={{0,8},{1,9},{2,10},{3,11},{4,12},{5,13},{6,14},{7,15},{8,0},{9,1},... | collective-permute-start | bytes 393224 | tf_op jit(solution)/shard_map/ppermute | solution.py:225
  69.5 6.8 %collective-permute-done.18.other_ref = bf16[64,1024]{1,0:T(8,128)(2,1)S(1)} collective-permute-done((bf16[64,1024]{1,0:T(8,128)(2,1)S(1)}, bf16[64,1024]{1,0:T(8,128)(2,1)S(1)}, u32[]{:S(2)}, u32[]{:S(2)}) %collective-permute-start.18) | collective-permute-done | bytes 131104 | tf_op jit(solution)/shard_map/ppermute | solution.py:225
  79.7 2.8 %collective-permute-done.20 = bf16[8,32,128]{2,1,0:T(8,128)(2,1)S(1)} collective-permute-done((bf16[8,32,128]{2,1,0:T(8,128)(2,1)S(1)}, bf16[8,32,128]{2,1,0:T(8,128)(2,1)S(1)}, u32[]{:S(2)}, u32[]{:S(2)}) %collective-permute-start.20) | collective-permute-done | bytes 65568 | tf_op jit(solution)/shard_map/ppermute | solution.py:225
  83.9 2.9 %collective-permute-done.21 = bf16[8,32,128]{2,1,0:T(8,128)(2,1)S(1)} collective-permute-done((bf16[8,32,128]{2,1,0:T(8,128)(2,1)S(1)}, bf16[8,32,128]{2,1,0:T(8,128)(2,1)S(1)}, u32[]{:S(2)}, u32[]{:S(2)}) %collective-permute-start.21) | collective-permute-done | bytes 65568 | tf_op jit(solution)/shard_map/ppermute | solution.py:225
  87.5 3.7 %collective-permute-done.22.other_ref = bf16[8,32,128]{2,1,0:T(8,128)(2,1)S(1)} collective-permute-done((bf16[8,32,128]{2,1,0:T(8,128)(2,1)S(1)}, bf16[8,32,128]{2,1,0:T(8,128)(2,1)S(1)}, u32[]{:S(2)}, u32[]{:S(2)}) %collective-permute-start.22) | collective-permute-done | bytes 65568 | tf_op jit(solution)/shard_map/ppermute | solution.py:225
  93.4 2.0 %collective-permute-start.24 = (bf16[64,1024]{1,0:T(8,128)(2,1)S(1)}, bf16[64,1024]{1,0:T(8,128)(2,1)S(1)}, u32[]{:S(2)}, u32[]{:S(2)}) collective-permute-start(bf16[64,1024]{1,0:T(8,128)(2,1)S(1)} %get-tuple-element.67), channel_id=1, source_target_pairs={{0,8},{1,9},{2,10},{3,11},{4,12},{5,13},{6,14},{7,15},{8,0},{9,1},... | collective-permute-start | bytes 393224 | tf_op jit(solution)/shard_map/ppermute | solution.py:225
  95.4 7.3 %collective-permute-done.24.other_ref = bf16[64,1024]{1,0:T(8,128)(2,1)S(1)} collective-permute-done((bf16[64,1024]{1,0:T(8,128)(2,1)S(1)}, bf16[64,1024]{1,0:T(8,128)(2,1)S(1)}, u32[]{:S(2)}, u32[]{:S(2)}) %collective-permute-start.24) | collective-permute-done | bytes 131104 | tf_op jit(solution)/shard_map/ppermute | solution.py:225
  103.5 3.6 %collective-permute-done.25 = f32[4,128]{1,0:T(4,128)S(1)} collective-permute-done((f32[4,128]{1,0:T(4,128)S(1)}, f32[4,128]{1,0:T(4,128)S(1)}, u32[]{:S(2)}, u32[]{:S(2)}) %collective-permute-start.25) | collective-permute-done | bytes 2080 | tf_op jit(solution)/shard_map/ppermute | solution.py:225
  107.9 2.8 %collective-permute-done.26 = f32[2,128]{1,0:T(2,128)S(1)} collective-permute-done((f32[2,128]{1,0:T(2,128)S(1)}, f32[2,128]{1,0:T(2,128)S(1)}, u32[]{:S(2)}, u32[]{:S(2)}) %collective-permute-start.26) | collective-permute-done | bytes 1056 | tf_op jit(solution)/shard_map/ppermute | solution.py:225
  113.3 2.1 %collective-permute-done.28 = f32[1,128]{1,0:T(1,128)S(1)} collective-permute-done((f32[1,128]{1,0:T(1,128)S(1)}, f32[1,128]{1,0:T(1,128)S(1)}, u32[]{:S(2)}, u32[]{:S(2)}) %collective-permute-start.28) | collective-permute-done | bytes 544 | tf_op jit(solution)/shard_map/ppermute | solution.py:225
  (75 shorter events, 31.9 us)
Async XLA Ops:
  1.6 16.0 %collective-permute-start.1 = (bf16[2,512,128]{2,1,0:T(8,128)(2,1)S(1)}, bf16[2,512,128]{2,1,0:T(8,128)(2,1)S(1)}, u32[]{:S(2)}, u32[]{:S(2)}) collective-permute-start(bf16[2,512,128]{2,1,0:T(8,128)(2,1)S(1)} %get-tuple-element.42), channel_id=1, source_target_pairs={{0,1},{1,0},{2,3},{3,2},{4,5},{5,4},{6,7},{7,6},{8,9},{9,8},{10,11... | collective-permute-start | bytes 786440 | tf_op jit(solution)/shard_map/ppermute | solution.py:225
  2.2 17.0 %collective-permute-start.2 = (bf16[2,512,128]{2,1,0:T(8,128)(2,1)S(1)}, bf16[2,512,128]{2,1,0:T(8,128)(2,1)S(1)}, u32[]{:S(2)}, u32[]{:S(2)}) collective-permute-start(bf16[2,512,128]{2,1,0:T(8,128)(2,1)S(1)} %get-tuple-element.43), channel_id=1, source_target_pairs={{0,2},{1,3},{2,0},{3,1},{4,6},{5,7},{6,4},{7,5},{8,10},{9,11},{10,... | collective-permute-start | bytes 786440 | tf_op jit(solution)/shard_map/ppermute | solution.py:225
  6.7 3.8 %collective-permute-start.8 = (bf16[2,48,128]{2,1,0:T(8,128)(2,1)S(1)}, bf16[2,48,128]{2,1,0:T(8,128)(2,1)S(1)}, u32[]{:S(2)}, u32[]{:S(2)}) collective-permute-start(bf16[2,48,128]{2,1,0:T(8,128)(2,1)S(1)} %shard_map.67.left_ref), channel_id=1, source_target_pairs={{0,16},{1,17},{2,18},{3,19},{4,20},{5,21},{6,22},{7,23},{8,24},{9,... | collective-permute-start | bytes 73736 | tf_op jit(solution)/shard_map/ppermute | solution.py:225
  10.6 4.2 %collective-permute-start.10 = (bf16[4,48,128]{2,1,0:T(8,128)(2,1)S(1)}, bf16[4,48,128]{2,1,0:T(8,128)(2,1)S(1)}, u32[]{:S(2)}, u32[]{:S(2)}) collective-permute-start(bf16[4,48,128]{2,1,0:T(8,128)(2,1)S(1)} %shard_map.68.refs_9_.refs_0_), channel_id=1, source_target_pairs={{0,4},{1,5},{2,6},{3,7},{4,0},{5,1},{6,2},{7,3},{8,12},{9,13},{10,... | collective-permute-start | bytes 147464 | tf_op jit(solution)/shard_map/ppermute | solution.py:225
  12.1 5.1 %collective-permute-start.11 = (bf16[4,48,128]{2,1,0:T(8,128)(2,1)S(1)}, bf16[4,48,128]{2,1,0:T(8,128)(2,1)S(1)}, u32[]{:S(2)}, u32[]{:S(2)}) collective-permute-start(bf16[4,48,128]{2,1,0:T(8,128)(2,1)S(1)} %shard_map.68.refs_9_.refs_0_), channel_id=1, source_target_pairs={{0,6},{1,7},{2,4},{3,5},{4,2},{5,3},{6,0},{7,1},{8,14},{9,15},{10,... | collective-permute-start | bytes 147464 | tf_op jit(solution)/shard_map/ppermute | solution.py:225
  12.2 5.4 %collective-permute-start.9 = (bf16[4,48,128]{2,1,0:T(8,128)(2,1)S(1)}, bf16[4,48,128]{2,1,0:T(8,128)(2,1)S(1)}, u32[]{:S(2)}, u32[]{:S(2)}) collective-permute-start(bf16[4,48,128]{2,1,0:T(8,128)(2,1)S(1)} %shard_map.68.refs_9_.refs_0_), channel_id=1, source_target_pairs={{0,2},{1,3},{2,0},{3,1},{4,6},{5,7},{6,4},{7,5},{8,10},{9,11},{10,... | collective-permute-start | bytes 147464 | tf_op jit(solution)/shard_map/ppermute | solution.py:225
  14.8 7.8 %collective-permute-start.3 = (bf16[2,512,128]{2,1,0:T(8,128)(2,1)S(1)}, bf16[2,512,128]{2,1,0:T(8,128)(2,1)S(1)}, u32[]{:S(2)}, u32[]{:S(2)}) collective-permute-start(bf16[2,512,128]{2,1,0:T(8,128)(2,1)S(1)} %get-tuple-element.44), channel_id=1, source_target_pairs={{0,3},{1,2},{2,1},{3,0},{4,7},{5,6},{6,5},{7,4},{8,11},{9,10},{10,... | collective-permute-start | bytes 786440 | tf_op jit(solution)/shard_map/ppermute | solution.py:225
  17.2 9.2 %collective-permute-start.4 = (bf16[2,512,128]{2,1,0:T(8,128)(2,1)S(1)}, bf16[2,512,128]{2,1,0:T(8,128)(2,1)S(1)}, u32[]{:S(2)}, u32[]{:S(2)}) collective-permute-start(bf16[2,512,128]{2,1,0:T(8,128)(2,1)S(1)} %get-tuple-element.45), channel_id=1, source_target_pairs={{0,4},{1,5},{2,6},{3,7},{4,0},{5,1},{6,2},{7,3},{8,12},{9,13},{10,... | collective-permute-start | bytes 786440 | tf_op jit(solution)/shard_map/ppermute | solution.py:225
  17.6 12.3 %collective-permute-start.5 = (bf16[2,512,128]{2,1,0:T(8,128)(2,1)S(1)}, bf16[2,512,128]{2,1,0:T(8,128)(2,1)S(1)}, u32[]{:S(2)}, u32[]{:S(2)}) collective-permute-start(bf16[2,512,128]{2,1,0:T(8,128)(2,1)S(1)} %get-tuple-element.46), channel_id=1, source_target_pairs={{0,5},{1,4},{2,7},{3,6},{4,1},{5,0},{6,3},{7,2},{8,13},{9,12},{10,... | collective-permute-start | bytes 786440 | tf_op jit(solution)/shard_map/ppermute | solution.py:225
  17.6 19.9 %collective-permute-start.6 = (bf16[2,512,128]{2,1,0:T(8,128)(2,1)S(1)}, bf16[2,512,128]{2,1,0:T(8,128)(2,1)S(1)}, u32[]{:S(2)}, u32[]{:S(2)}) collective-permute-start(bf16[2,512,128]{2,1,0:T(8,128)(2,1)S(1)} %get-tuple-element.47), channel_id=1, source_target_pairs={{0,6},{1,7},{2,4},{3,5},{4,2},{5,3},{6,0},{7,1},{8,14},{9,15},{10,... | collective-permute-start | bytes 786440 | tf_op jit(solution)/shard_map/ppermute | solution.py:225
  19.2 20.5 %collective-permute-start = (bf16[2,512,128]{2,1,0:T(8,128)(2,1)S(1)}, bf16[2,512,128]{2,1,0:T(8,128)(2,1)S(1)}, u32[]{:S(2)}, u32[]{:S(2)}) collective-permute-start(bf16[2,512,128]{2,1,0:T(8,128)(2,1)S(1)} %get-tuple-element.37), channel_id=1, source_target_pairs={{0,7},{1,6},{2,5},{3,4},{4,3},{5,2},{6,1},{7,0},{8,15},{9,14},{10,... | collective-permute-start | bytes 786440 | tf_op jit(solution)/shard_map/ppermute | solution.py:225
  40.2 9.6 %collective-permute-start.12 = (bf16[64,1024]{1,0:T(8,128)(2,1)S(1)}, bf16[64,1024]{1,0:T(8,128)(2,1)S(1)}, u32[]{:S(2)}, u32[]{:S(2)}) collective-permute-start(bf16[64,1024]{1,0:T(8,128)(2,1)S(1)} %get-tuple-element.56), channel_id=1, source_target_pairs={{0,8},{1,9},{2,10},{3,11},{4,12},{5,13},{6,14},{7,15},{8,0},{9,1},... | collective-permute-start | bytes 393224 | tf_op jit(solution)/shard_map/ppermute | solution.py:225
  50.2 1.3 %collective-permute-start.13 = (bf16[8,32,128]{2,1,0:T(8,128)(2,1)S(1)}, bf16[8,32,128]{2,1,0:T(8,128)(2,1)S(1)}, u32[]{:S(2)}, u32[]{:S(2)}) collective-permute-start(bf16[8,32,128]{2,1,0:T(8,128)(2,1)S(1)} %get-tuple-element.59), channel_id=1, source_target_pairs={{0,1},{1,0},{2,3},{3,2},{4,5},{5,4},{6,7},{7,6},{8,9},{9,8},{10,11... | collective-permute-start | bytes 196616 | tf_op jit(solution)/shard_map/ppermute | solution.py:225
  51.6 4.4 %collective-permute-start.14 = (bf16[8,32,128]{2,1,0:T(8,128)(2,1)S(1)}, bf16[8,32,128]{2,1,0:T(8,128)(2,1)S(1)}, u32[]{:S(2)}, u32[]{:S(2)}) collective-permute-start(bf16[8,32,128]{2,1,0:T(8,128)(2,1)S(1)} %fusion), channel_id=1, source_target_pairs={{0,16},{1,17},{2,18},{3,19},{4,20},{5,21},{6,22},{7,23},{8,24},{9,... | collective-permute-start | bytes 196616 | tf_op jit(solution)/shard_map/ppermute | solution.py:225
  56.1 4.3 %collective-permute-start.15 = (bf16[8,32,128]{2,1,0:T(8,128)(2,1)S(1)}, bf16[8,32,128]{2,1,0:T(8,128)(2,1)S(1)}, u32[]{:S(2)}, u32[]{:S(2)}) collective-permute-start(bf16[8,32,128]{2,1,0:T(8,128)(2,1)S(1)} %fusion.2), channel_id=1, source_target_pairs={{0,2},{1,3},{2,0},{3,1},{4,6},{5,7},{6,4},{7,5},{8,10},{9,11},{10,... | collective-permute-start | bytes 196616 | tf_op jit(solution)/shard_map/ppermute | solution.py:225
  60.4 4.3 %collective-permute-start.16 = (bf16[8,32,128]{2,1,0:T(8,128)(2,1)S(1)}, bf16[8,32,128]{2,1,0:T(8,128)(2,1)S(1)}, u32[]{:S(2)}, u32[]{:S(2)}) collective-permute-start(bf16[8,32,128]{2,1,0:T(8,128)(2,1)S(1)} %get-tuple-element.71), channel_id=1, source_target_pairs={{0,4},{1,5},{2,6},{3,7},{4,0},{5,1},{6,2},{7,3},{8,12},{9,13},{10,... | collective-permute-start | bytes 196616 | tf_op jit(solution)/shard_map/ppermute | solution.py:225
  67.0 9.3 %collective-permute-start.18 = (bf16[64,1024]{1,0:T(8,128)(2,1)S(1)}, bf16[64,1024]{1,0:T(8,128)(2,1)S(1)}, u32[]{:S(2)}, u32[]{:S(2)}) collective-permute-start(bf16[64,1024]{1,0:T(8,128)(2,1)S(1)} %get-tuple-element.63), channel_id=1, source_target_pairs={{0,8},{1,9},{2,10},{3,11},{4,12},{5,13},{6,14},{7,15},{8,0},{9,1},... | collective-permute-start | bytes 393224 | tf_op jit(solution)/shard_map/ppermute | solution.py:225
  78.1 4.3 %collective-permute-start.20 = (bf16[8,32,128]{2,1,0:T(8,128)(2,1)S(1)}, bf16[8,32,128]{2,1,0:T(8,128)(2,1)S(1)}, u32[]{:S(2)}, u32[]{:S(2)}) collective-permute-start(bf16[8,32,128]{2,1,0:T(8,128)(2,1)S(1)} %fusion.1), channel_id=1, source_target_pairs={{0,16},{1,17},{2,18},{3,19},{4,20},{5,21},{6,22},{7,23},{8,24},{9,... | collective-permute-start | bytes 196616 | tf_op jit(solution)/shard_map/ppermute | solution.py:225
  82.5 4.3 %collective-permute-start.21 = (bf16[8,32,128]{2,1,0:T(8,128)(2,1)S(1)}, bf16[8,32,128]{2,1,0:T(8,128)(2,1)S(1)}, u32[]{:S(2)}, u32[]{:S(2)}) collective-permute-start(bf16[8,32,128]{2,1,0:T(8,128)(2,1)S(1)} %fusion.3), channel_id=1, source_target_pairs={{0,2},{1,3},{2,0},{3,1},{4,6},{5,7},{6,4},{7,5},{8,10},{9,11},{10,... | collective-permute-start | bytes 196616 | tf_op jit(solution)/shard_map/ppermute | solution.py:225
  86.9 4.3 %collective-permute-start.22 = (bf16[8,32,128]{2,1,0:T(8,128)(2,1)S(1)}, bf16[8,32,128]{2,1,0:T(8,128)(2,1)S(1)}, u32[]{:S(2)}, u32[]{:S(2)}) collective-permute-start(bf16[8,32,128]{2,1,0:T(8,128)(2,1)S(1)} %get-tuple-element.69), channel_id=1, source_target_pairs={{0,4},{1,5},{2,6},{3,7},{4,0},{5,1},{6,2},{7,3},{8,12},{9,13},{10,... | collective-permute-start | bytes 196616 | tf_op jit(solution)/shard_map/ppermute | solution.py:225
  93.4 9.3 %collective-permute-start.24 = (bf16[64,1024]{1,0:T(8,128)(2,1)S(1)}, bf16[64,1024]{1,0:T(8,128)(2,1)S(1)}, u32[]{:S(2)}, u32[]{:S(2)}) collective-permute-start(bf16[64,1024]{1,0:T(8,128)(2,1)S(1)} %get-tuple-element.67), channel_id=1, source_target_pairs={{0,8},{1,9},{2,10},{3,11},{4,12},{5,13},{6,14},{7,15},{8,0},{9,1},... | collective-permute-start | bytes 393224 | tf_op jit(solution)/shard_map/ppermute | solution.py:225
  103.4 3.7 %collective-permute-start.25 = (f32[4,128]{1,0:T(4,128)S(1)}, f32[4,128]{1,0:T(4,128)S(1)}, u32[]{:S(2)}, u32[]{:S(2)}) collective-permute-start(f32[4,128]{1,0:T(4,128)S(1)} %slice.19), channel_id=1, source_target_pairs={{0,4},{1,5},{2,6},{3,7},{4,0},{5,1},{6,2},{7,3},{8,12},{9,13},{10,... | collective-permute-start | bytes 6152 | tf_op jit(solution)/shard_map/ppermute | solution.py:225
  107.1 3.6 %collective-permute-start.26 = (f32[2,128]{1,0:T(2,128)S(1)}, f32[2,128]{1,0:T(2,128)S(1)}, u32[]{:S(2)}, u32[]{:S(2)}) collective-permute-start(f32[2,128]{1,0:T(2,128)S(1)} %slice.21), channel_id=1, source_target_pairs={{0,2},{1,3},{2,0},{3,1},{4,6},{5,7},{6,4},{7,5},{8,10},{9,11},{10,... | collective-permute-start | bytes 3080 | tf_op jit(solution)/shard_map/ppermute | solution.py:225
  111.8 3.6 %collective-permute-start.28 = (f32[1,128]{1,0:T(1,128)S(1)}, f32[1,128]{1,0:T(1,128)S(1)}, u32[]{:S(2)}, u32[]{:S(2)}) collective-permute-start(f32[1,128]{1,0:T(1,128)S(1)} %slice_add_fusion.2), channel_id=1, source_target_pairs={{0,16},{1,17},{2,18},{3,19},{4,20},{5,21},{6,22},{7,23},{8,24},{9,... | collective-permute-start | bytes 1544 | tf_op jit(solution)/shard_map/ppermute | solution.py:225
  (9 other events, 44.3 us)
